TPU v7x, 128 devices: a whole 4x4x4 slice. The times are simulated.
128 devices in a mesh: seq: 16 (over z, x), head: 8 (over y, core).
Axes of the slice: x: 4, y: 4, z: 4, core: 2. Of those that a mesh axis runs over, the one named last changes fastest.
Arguments:
- x_inputs: bfloat16 [131072, 1024], P('seq', 'head'), may hold values from -6 to 6
- x_in_proj: bfloat16 [131072, 128], P('seq'), may hold values from -0.5 to 0.5
- x_out_proj: bfloat16 [131072, 128], P('seq'), may hold values from -6 to 6
- x_log_decay: float32 [16, 131072], P('head', 'seq'), may hold values from -0.6 to 0
- x_step: float32 [16, 131072], P('head', 'seq'), may hold values from 0 to 0.5
- z_source: int32 [131072], P('seq'), may hold values from 0 to 131071, as said below
- z_in_proj: bfloat16 [131072, 128], P('seq'), may hold values from -0.5 to 0.5
- z_out_proj: bfloat16 [131072, 128], P('seq'), may hold values from -6 to 6
- z_log_decay: float32 [16, 131072], P('head', 'seq'), may hold values from -0.6 to 0
- z_step: float32 [16, 131072], P('head', 'seq'), may hold values from 0 to 0.5
- gate_branch: bfloat16 [131072, 1024], P('seq', 'head'), may hold values from -8 to 8
- norm_gain: float32 [1024], P('head'), may hold values from 0.1 to 1.9
- out_weight: bfloat16 [1024, 512], P('head'), may hold values from -0.1875 to 0.1875
Outputs:
- layer_out: bfloat16 [131072, 512], P(('seq', 'head'))
Inputs may be any that keep to these rules, and one draw needn't show every extreme that they name: z_source is a permutation; every block of 8192 consecutive z-order positions takes exactly 512 tokens from each block of 8192 consecutive x-order tokens.
All inputs are finite; a program needn't handle non-finite values.
Results may differ from a plain program's by a relative error of at most 0.034.
Values may be sent and summed in bfloat16 or wider, within the bound.
No kernel may reach another device: no remote copies, remote signals or barrier semaphores. Data moves between devices by JAX's collectives and lax.ppermute only.
A program may use at most 128 MiB of HBM per device.

v0:
```python
import jax
import jax.numpy as jnp
from jax import lax
from jax.sharding import PartitionSpec as P

BLOCK = 512


def shifted(value, axis, steps):
    count = lax.axis_size(axis)
    initial, last = (max(0, -steps), min(count, count - steps))
    return lax.ppermute(value, axis, [(source, source + steps) for source in range(initial, last)])


def local_blocks(inputs, b_mat, c_mat, log_decay, step):
    count = inputs.shape[0]
    blocks = count // BLOCK
    heads = log_decay.shape[0]
    width = inputs.shape[1]
    head_width = width // heads
    state = b_mat.shape[1]
    cum = jnp.cumsum(log_decay.reshape(heads, blocks, BLOCK), axis=2).transpose(1, 0, 2)
    totals = cum[:, :, -1]
    step_blocks = step.reshape(heads, blocks, BLOCK).transpose(1, 0, 2)
    u_blocks = inputs.reshape(blocks, BLOCK, heads, head_width)
    b_blocks = b_mat.reshape(blocks, BLOCK, state)
    c_blocks = c_mat.reshape(blocks, BLOCK, state)
    rows = lax.broadcasted_iota(jnp.int32, (BLOCK, BLOCK), 0)
    cols = lax.broadcasted_iota(jnp.int32, (BLOCK, BLOCK), 1)
    lower = rows >= cols

    def one_block(carry, pieces):
        u_blk, b_blk, c_blk, cum_blk, d_blk, tot_blk = pieces
        scores = jnp.dot(c_blk, b_blk.T, preferred_element_type=jnp.float32)
        diff = jnp.where(lower[None], cum_blk[:, :, None] - cum_blk[:, None, :], -jnp.inf)
        weights = (scores[None] * jnp.exp(diff) * d_blk[:, None, :]).astype(jnp.bfloat16)
        intra = jnp.einsum("hts,shp->thp", weights, u_blk, preferred_element_type=jnp.float32)
        scale = (jnp.exp(tot_blk[:, None] - cum_blk) * d_blk).T
        contrib = (u_blk * scale[:, :, None]).astype(jnp.bfloat16)
        state_add = jnp.einsum("shp,sn->hpn", contrib, b_blk, preferred_element_type=jnp.float32)
        updated = jnp.exp(tot_blk)[:, None, None] * carry + state_add
        return (updated, (intra, carry))

    start = jnp.zeros((heads, head_width, state), jnp.float32)
    final, (intra_all, local_in) = lax.scan(
        one_block, start, (u_blocks, b_blocks, c_blocks, cum, step_blocks, totals)
    )
    return (intra_all, local_in, final, cum, totals, c_blocks)


def incoming_state(device_decay, final):

    def relay(index, pair):
        received = shifted(pair[1].astype(jnp.bfloat16), "seq", 1).astype(jnp.float32)
        return (received, device_decay[:, None, None] * received + final)

    start, _ = lax.fori_loop(0, lax.axis_size("seq") - 1, relay, (jnp.zeros_like(final), final))
    return start


def ssd_scan(inputs, b_mat, c_mat, log_decay, step):
    intra_all, local_in, final, cum, totals, c_blocks = local_blocks(
        inputs, b_mat, c_mat, log_decay, step
    )
    device_decay = jnp.exp(jnp.sum(totals, axis=0))
    start = incoming_state(device_decay, final)
    before = jnp.cumsum(totals, axis=0) - totals
    carried = local_in + jnp.exp(before)[:, :, None, None] * start[None]
    inter = jnp.einsum(
        "bqn,bhpn->bqhp", c_blocks, carried.astype(jnp.bfloat16), preferred_element_type=jnp.float32
    )
    inter = inter * jnp.exp(cum).transpose(0, 2, 1)[:, :, :, None]
    return (intra_all + inter).astype(jnp.bfloat16).reshape(inputs.shape)


def body(
    x_inputs,
    x_in_proj,
    x_out_proj,
    x_log_decay,
    x_step,
    z_source,
    z_in_proj,
    z_out_proj,
    z_log_decay,
    z_step,
    gate_branch,
    norm_gain,
    out_weight,
):
    y_x = ssd_scan(x_inputs, x_in_proj, x_out_proj, x_log_decay, x_step)
    whole = lax.all_gather(y_x, "seq", axis=0, tiled=True)
    u_z = jnp.take(whole, z_source, axis=0)
    y_z = ssd_scan(u_z, z_in_proj, z_out_proj, z_log_decay, z_step)
    gated = y_z.astype(jnp.float32) * jax.nn.silu(gate_branch.astype(jnp.float32))
    squares = lax.psum(jnp.sum(gated * gated, axis=1).astype(jnp.bfloat16), "head").astype(
        jnp.float32
    )
    mean_square = squares / (gated.shape[1] * lax.axis_size("head"))
    normed = (gated * lax.rsqrt(mean_square[:, None] + 1e-05) * norm_gain).astype(jnp.bfloat16)
    return lax.psum_scatter(
        jnp.dot(normed, out_weight, preferred_element_type=jnp.float32).astype(jnp.bfloat16),
        "head",
        scatter_dimension=0,
        tiled=True,
    )


def solution(mesh):
    placed = (
        P("seq", "head"),
        P("seq", None),
        P("seq", None),
        P("head", "seq"),
        P("head", "seq"),
        P("seq"),
        P("seq", None),
        P("seq", None),
        P("head", "seq"),
        P("head", "seq"),
        P("seq", "head"),
        P("head"),
        P("head", None),
    )
    return jax.shard_map(
        body, mesh=mesh, in_specs=placed, out_specs=P(("seq", "head"), None), check_vma=False
    )
```

profile of v0, /device:TPU:1, one launch (start us, length us, event | category | flops | bytes accessed | tf_op | source)
XLA Modules:
  0.0 932.3 jit_solution(13976984456812221220)
XLA Ops:
  14.1 8.2 reshape.159
  22.3 10.6 %copy.53 = bf16[16,512,2,64]{1,3,2,0:T(8,128)(2,1)} copy(bf16[16,512,2,64]{3,2,1,0:T(2,128)(2,1)} %reshape.159) | data formatting | bytes 4194304
  35.5 93.9 %while.56 = (s32[]{:T(128)}, f32[2,64,128]{2,1,0:T(8,128)S(1)}, f32[16,512,2,64]{1,3,2,0:T(8,128)}, f32[16,2,64,128]{3,2,1,0:T(8,128)S(1)}, f32[16,2]{1,0:T(8,12...) while((s32[]{:T(128)}, f32[2,64,128]{2,1,0:T(8,128)S(1)}, ...), condition=%wide.region_3.4_spmd.clone, body=%wide.region_2.3_spmd.clone.sunk | while | flops 154142720 | bytes 3853496 | solution.py:45
  130.2 101.2 %while.54 = (s32[]{:T(128)}, f32[2,64,128]{2,1,0:T(8,128)}, bf16[2,64,128]{2,1,0:T(8,128)(2,1)S(1)}, f32[2]{0:T(128)S(1)}, f32[2,64,128]{2,1,0:T(8,128)S(1)}, /*index=5*/s32[]{:T(128)}) while((s32[]{:T(128)}, f32[2,64,128]{2,1,0:T(8,128)}, bf16[2,64,128]{2,1,0:T(8,128)(2,1)S(1)}, f32[2]{0:T(128)S(1)}, f32[2,64,128]{2,1,0:T(8,128)S(1)}, ...), condition=%wide.region_7.8_spmd, body=%wide.region_6.7_spmd.sunk | while | flops 65538 | bytes 327797 | solution.py:57
  130.2 3.9 collective-permute-start
  135.7 3.6 collective-permute-start
  141.0 3.6 collective-permute-start
  146.3 3.6 collective-permute-start
  151.6 4.2 collective-permute-start
  157.4 5.7 collective-permute-start
  164.8 5.7 collective-permute-start
  172.2 5.7 collective-permute-start
  179.6 5.9 collective-permute-start
  187.1 5.6 collective-permute-start
  194.4 5.7 collective-permute-start
  201.8 5.7 collective-permute-start
  209.2 5.7 collective-permute-start
  216.6 5.7 collective-permute-start
  224.0 5.7 collective-permute-start
  231.4 3.6 fusion.59
  235.0 7.3 copy.73
  242.3 7.8 reshape.160
  251.2 2.9 copy.68
  254.2 221.1 %all-gather.2.cloned.1.call-done = bf16[131072,128]{1,0:T(8,128)(2,1)} async-done(((bf16[8192,128]{1,0:T(8,128)(2,1)}), bf16[131072,128]{1,0:T(8,128)(2,1)}) %all-gather.2.cloned.1.call-update) | async-done | bytes 33554448 | tf_op jit(solution)/shard_map/all_gather | solution.py:92
  475.3 122.0 %gather_fusion = bf16[8192,128]{1,0:T(8,128)(2,1)} fusion(bf16[131072,128]{1,0:T(8,128)(2,1)} %all-gather.2.cloned.1.call-done, s32[8192]{0:T(1024)S(1)} %fusion.69), kind=kCustom, calls=%fused_computation | custom fusion | bytes 4227072 | tf_op jit(solution)/shard_map/jit(_take)/gather | solution.py:93
  597.3 4.1 copy.60
  609.1 93.9 %while.57 = (s32[]{:T(128)}, f32[2,64,128]{2,1,0:T(8,128)S(1)}, f32[16,512,2,64]{1,3,2,0:T(8,128)}, f32[16,2,64,128]{3,2,1,0:T(8,128)S(1)}, f32[16,2]{1,0:T(8,12...) while((s32[]{:T(128)}, f32[2,64,128]{2,1,0:T(8,128)S(1)}, ...), condition=%wide.region_11.12_spmd.clone, body=%wide.region_10.11_spmd.clone.sunk | while | flops 154142720 | bytes 3853496 | solution.py:45
  703.7 99.8 %while.55 = (s32[]{:T(128)}, f32[2,64,128]{2,1,0:T(8,128)}, bf16[2,64,128]{2,1,0:T(8,128)(2,1)S(1)}, f32[2]{0:T(128)S(1)}, f32[2,64,128]{2,1,0:T(8,128)S(1)}, /*index=5*/s32[]{:T(128)}) while((s32[]{:T(128)}, f32[2,64,128]{2,1,0:T(8,128)}, bf16[2,64,128]{2,1,0:T(8,128)(2,1)S(1)}, f32[2]{0:T(128)S(1)}, f32[2,64,128]{2,1,0:T(8,128)S(1)}, ...), condition=%wide.region_15.16_spmd, body=%wide.region_14.15_spmd.sunk | while | flops 65538 | bytes 327797 | solution.py:57
  703.7 3.3 collective-permute-start.1
  708.6 3.6 collective-permute-start.1
  713.9 3.6 collective-permute-start.1
  719.1 3.6 collective-permute-start.1
  724.4 3.6 collective-permute-start.1
  729.7 5.6 collective-permute-start.1
  737.0 5.7 collective-permute-start.1
  744.4 5.7 collective-permute-start.1
  751.8 5.9 collective-permute-start.1
  759.3 5.6 collective-permute-start.1
  766.6 5.7 collective-permute-start.1
  773.9 5.7 collective-permute-start.1
  781.3 5.7 collective-permute-start.1
  788.7 5.7 collective-permute-start.1
  796.1 5.7 collective-permute-start.1
  803.5 3.6 fusion.62
  809.6 3.4 copy.82
  816.4 36.8 %psum.7 = bf16[8192]{0:T(1024)(128)(2,1)S(1)} all-reduce(bf16[8192]{0:T(1024)(128)(2,1)S(1)} %multiply_reduce_fusion), channel_id=1, replica_groups=mesh['seq'=16,'head'=8] {'head'}, use_global_device_ids=true, to_apply=%region_17.18 | all-reduce | flops 8192 | bytes 32768 | tf_op jit(solution)/shard_map/psum | solution.py:96
  853.2 8.6 convolution_convert_fusion
  861.9 63.6 %reduce-scatter.2.cloned.1.call-done = bf16[1024,512]{1,0:T(8,128)(2,1)} async-done(((bf16[8192,512]{1,0:T(8,128)(2,1)}), bf16[1024,512]{1,0:T(8,128)(2,1)}) %reduce-scatter.2.cloned.1.call-update) | async-done | bytes 1048592 | tf_op jit(solution)/shard_map/reduce_scatter | solution.py:101
  (406 shorter events, 261.3 us)
Async XLA Ops:
  6.5 846.7 %copy-start = (bf16[128,512]{1,0:T(8,128)(2,1)S(1)}, bf16[128,512]{1,0:T(8,128)(2,1)}, u32[]{:S(2)}) copy-start(bf16[128,512]{1,0:T(8,128)(2,1)} %param.33) | copy-start | bytes 393220
  6.5 468.8 %all-gather.2.cloned.1.call-start = ((), (), s32[]{:S(2)}) async-start(), calls=%async_computation.1 | async-start | bytes 35651584 | tf_op jit(solution)/shard_map/all_gather | solution.py:92
  130.2 4.9 collective-permute-start
  135.7 4.6 collective-permute-start
  141.0 4.6 collective-permute-start
  146.3 4.6 collective-permute-start
  151.6 5.2 collective-permute-start
  157.4 6.8 collective-permute-start
  164.8 6.8 collective-permute-start
  172.2 6.8 collective-permute-start
  179.6 6.9 collective-permute-start
  187.1 6.6 collective-permute-start
  194.4 6.8 collective-permute-start
  201.8 6.8 collective-permute-start
  209.2 6.8 collective-permute-start
  216.6 6.8 collective-permute-start
  224.0 6.8 collective-permute-start
  250.0 0.8 copy-start.2
  250.1 675.4 %reduce-scatter.2.cloned.1.call-start = ((), (), s32[]{:S(2)}) async-start(), calls=%async_computation.2 | async-start | bytes 9437184 | tf_op jit(solution)/shard_map/reduce_scatter | solution.py:101
  703.7 4.3 collective-permute-start.1
  708.6 4.6 collective-permute-start.1
  713.9 4.6 collective-permute-start.1
  719.1 4.6 collective-permute-start.1
  724.4 4.6 collective-permute-start.1
  729.7 6.6 collective-permute-start.1
  737.0 6.8 collective-permute-start.1
  744.4 6.8 collective-permute-start.1
  751.8 6.9 collective-permute-start.1
  759.3 6.6 collective-permute-start.1
  766.6 6.8 collective-permute-start.1
  773.9 6.8 collective-permute-start.1
  781.3 6.8 collective-permute-start.1
  788.7 6.8 collective-permute-start.1
  796.1 6.8 collective-permute-start.1
  813.0 2.0 copy-start.1
  814.9 38.3 %copy-start.3 = (f32[128]{0:T(128)S(1)}, f32[128]{0:T(128)}, u32[]{:S(2)}) copy-start(f32[128]{0:T(128)} %param.32) | copy-start | bytes 1540
Sparse Core Ops, SparseCore 0:
  250.2 225.0 all-gather.1
  862.0 63.4 reduce-scatter.1
where the time goes:
time: 938 us; the launch traced here: 932 us
  waiting for transfers between devices  315 us (34%)
  local copies, waits for them, and re-layouts  186 us (20%)
  matrix products  173 us (18%)
  starting transfers between devices  152 us (16%)
  other arithmetic  53.4 us (6%)
  blocking collectives  36.8 us (4%)
  between operations  13.6 us (1%)
    all_gather x1, waiting for transfers between devices, body(): whole = lax.all_gather(y_x, 'seq', axis=0, tiled=True)  221 us
    ppermute x30, starting transfers between devices, shifted(): lax.ppermute(value, axis, [(source, source + steps) for source in range(i...  152 us
    gather x2, local copies, waits for them, and re-layouts, body(): u_z = jnp.take(whole, z_source, axis=0)  126 us
    dot_general x32, matrix products, one_block(): jnp.einsum('hts,shp->thp', weights, u_blk, preferred_element_type=jnp.flo...  80.4 us
    reduce_scatter x1, waiting for transfers between devices, body(): lax.psum_scatter(jnp.dot(normed, out_weight, preferred_element_type=jnp.f...  63.6 us
    dot_general x32, matrix products, one_block(): scores = jnp.dot(c_blk, b_blk.T, preferred_element_type=jnp.float32)  40.4 us
    psum x1, blocking collectives, body(): lax.psum(jnp.sum(gated * gated, axis=1).astype(jnp.bfloat16), 'head')  36.8 us
    dot_general x32, matrix products, one_block(): jnp.einsum('shp,sn->hpn', contrib, b_blk, preferred_element_type=jnp.floa...  36.7 us
  transfers between devices with their start and end apart: 32, of which 32 were waited for; matrix products, arithmetic and copies ran while one was open for 0% of the time, Pallas kernels for 0%

commit v1 on v0

--- a/solution.py
+++ b/solution.py
@@ -89,7 +89,15 @@
     out_weight,
 ):
     y_x = ssd_scan(x_inputs, x_in_proj, x_out_proj, x_log_decay, x_step)
-    whole = lax.all_gather(y_x, "seq", axis=0, tiled=True)
+
+    def views_check(local, a_name):
+        u_next = lax.axis_size(a_name)
+        carry_in = jnp.stack(u_next * [local], 0)
+        outcome_arr = lax.all_to_all(carry_in, axis_name=a_name, split_axis=0, concat_axis=0)
+        f_now = jnp.concatenate(outcome_arr, 0)
+        return f_now
+
+    whole = views_check(y_x, "seq")
     u_z = jnp.take(whole, z_source, axis=0)
     y_z = ssd_scan(u_z, z_in_proj, z_out_proj, z_log_decay, z_step)
     gated = y_z.astype(jnp.float32) * jax.nn.silu(gate_branch.astype(jnp.float32))

time: 938 us -> 1230 us (1.31)
  waiting for transfers between devices: 315 us -> 552 us
  starting transfers between devices: 152 us -> 174 us
  blocking collectives: 36.8 us -> 55.2 us
    all_to_all x0 -> x1, waiting for transfers between devices: none -> 457 us  [views_check(): lax.all_to_all(carry_in, axis_name=a_name, split_axis=0, concat_axis=0)]
    all_gather x1 -> x0, waiting for transfers between devices: 221 us -> none  [body(): whole = lax.all_gather(y_x, 'seq', axis=0, tiled=True)]
    another operation x11 -> x14, local copies, waits for them, and re-layouts: 7.51 us -> 32.8 us  [the longest x3 25.3 us: views_check(): carry_in = jnp.stack(u_next * [local], 0)]
    psum x1, blocking collectives: 36.8 us -> 55.2 us  [body(): lax.psum(jnp.sum(gated * gated, axis=1).astype(jnp.bfloat16), 'head')]
    all_to_all x0 -> x1, starting transfers between devices: none -> 16.3 us  [views_check(): lax.all_to_all(carry_in, axis_name=a_name, split_axis=0, concat_axis=0)]
    reshape x4 -> x2, local copies, waits for them, and re-layouts: 16 us -> 0.95 us  [the longest x2 15.1 us: ssd_scan(): return (intra_all + inter).astype(jnp.bfloat16).reshape(inputs.shape)]
where the time goes in v1:
time: 1230 us; the launch traced here: 1220 us
  waiting for transfers between devices  552 us (45%)
  local copies, waits for them, and re-layouts  196 us (16%)
  starting transfers between devices  174 us (14%)
  matrix products  173 us (14%)
  blocking collectives  55.2 us (4%)
  other arithmetic  53.4 us (4%)
  between operations  13.7 us (1%)
    all_to_all x1, waiting for transfers between devices, views_check(): lax.all_to_all(carry_in, axis_name=a_name, split_axis=0, concat_axis=0)  457 us
    ppermute x30, starting transfers between devices, shifted(): lax.ppermute(value, axis, [(source, source + steps) for source in range(i...  157 us
    gather x2, local copies, waits for them, and re-layouts, body(): u_z = jnp.take(whole, z_source, axis=0)  126 us
    dot_general x32, matrix products, one_block(): jnp.einsum('hts,shp->thp', weights, u_blk, preferred_element_type=jnp.flo...  80.4 us
    reduce_scatter x1, waiting for transfers between devices, body(): lax.psum_scatter(jnp.dot(normed, out_weight, preferred_element_type=jnp.f...  64.9 us
    psum x1, blocking collectives, body(): lax.psum(jnp.sum(gated * gated, axis=1).astype(jnp.bfloat16), 'head')  55.2 us
    dot_general x32, matrix products, one_block(): scores = jnp.dot(c_blk, b_blk.T, preferred_element_type=jnp.float32)  40.4 us
    dot_general x32, matrix products, one_block(): jnp.einsum('shp,sn->hpn', contrib, b_blk, preferred_element_type=jnp.floa...  36.7 us
  transfers between devices with their start and end apart: 32, of which 32 were waited for; matrix products, arithmetic and copies ran while one was open for 0% of the time, Pallas kernels for 0%

profile of v1, /device:TPU:1, one launch (start us, length us, event | category | flops | bytes accessed | tf_op | source)
XLA Modules:
  0.0 1220.0 jit_solution(9132744668073512003)
XLA Ops:
  14.1 8.2 reshape.161
  22.3 10.6 copy.53
  35.5 93.9 %while.56 = (s32[]{:T(128)}, f32[2,64,128]{2,1,0:T(8,128)S(1)}, f32[16,512,2,64]{1,3,2,0:T(8,128)}, f32[16,2,64,128]{3,2,1,0:T(8,128)S(1)}, f32[16,2]{1,0:T(8,12...) while((s32[]{:T(128)}, f32[2,64,128]{2,1,0:T(8,128)S(1)}, ...), condition=%wide.region_3.4_spmd.clone, body=%wide.region_2.3_spmd.clone.sunk | while | flops 154142720 | bytes 3853496 | solution.py:45
  130.1 101.2 %while.54 = (s32[]{:T(128)}, f32[2,64,128]{2,1,0:T(8,128)}, bf16[2,64,128]{2,1,0:T(8,128)(2,1)S(1)}, f32[2]{0:T(128)S(1)}, f32[2,64,128]{2,1,0:T(8,128)S(1)}, /*index=5*/s32[]{:T(128)}) while((s32[]{:T(128)}, f32[2,64,128]{2,1,0:T(8,128)}, bf16[2,64,128]{2,1,0:T(8,128)(2,1)S(1)}, f32[2]{0:T(128)S(1)}, f32[2,64,128]{2,1,0:T(8,128)S(1)}, ...), condition=%wide.region_7.8_spmd, body=%wide.region_6.7_spmd.sunk | while | flops 65538 | bytes 327797 | solution.py:57
  130.1 3.9 collective-permute-start
  135.7 3.6 collective-permute-start
  141.0 3.6 collective-permute-start
  146.3 3.6 collective-permute-start
  151.6 4.2 collective-permute-start
  157.4 5.7 collective-permute-start
  164.8 5.7 collective-permute-start
  172.2 5.7 collective-permute-start
  179.6 5.9 collective-permute-start
  187.1 5.6 collective-permute-start
  194.4 5.7 collective-permute-start
  201.8 5.7 collective-permute-start
  209.2 5.7 collective-permute-start
  216.6 5.7 collective-permute-start
  224.0 5.7 collective-permute-start
  231.4 3.6 fusion.59
  235.0 7.3 copy.73
  242.3 6.8 reshape.162
  249.0 11.2 stack.3
  260.2 16.3 %all-to-all-start = ((bf16[16,8192,128]{2,1,0:T(8,128)(2,1)}), bf16[16,8192,128]{2,1,0:T(8,128)(2,1)}, u32[]{:S(2)}, u32[]{:S(2)}) async-start(bf16[16,8192,128]{2,1,0:T(8,128)(2,1)} %stack.3), calls=%async_computation | async-start | bytes 67108864 | tf_op jit(solution)/shard_map/all_to_all | solution.py:96
  280.2 457.3 %all-to-all-done = bf16[16,8192,128]{2,1,0:T(8,128)(2,1)} async-done(((bf16[16,8192,128]{2,1,0:T(8,128)(2,1)}), bf16[16,8192,128]{2,1,0:T(8,128)(2,1)}, u32[]{:S(2)}, u32[]{:S(2)}) %all-to-all-start) | async-done | bytes 33554464 | tf_op jit(solution)/shard_map/all_to_all | solution.py:96
  737.6 122.0 %gather_fusion = bf16[8192,128]{1,0:T(8,128)(2,1)} fusion(bf16[131072,128]{1,0:T(8,128)(2,1)} %bitcast.10, s32[8192]{0:T(1024)S(1)} %fusion.69), kind=kCustom, calls=%fused_computation | custom fusion | bytes 4227072 | tf_op jit(solution)/shard_map/jit(_take)/gather | solution.py:101
  859.5 4.1 copy.60
  871.3 93.9 %while.57 = (s32[]{:T(128)}, f32[2,64,128]{2,1,0:T(8,128)S(1)}, f32[16,512,2,64]{1,3,2,0:T(8,128)}, f32[16,2,64,128]{3,2,1,0:T(8,128)S(1)}, f32[16,2]{1,0:T(8,12...) while((s32[]{:T(128)}, f32[2,64,128]{2,1,0:T(8,128)S(1)}, ...), condition=%wide.region_11.12_spmd.clone, body=%wide.region_10.11_spmd.clone.sunk | while | flops 154142720 | bytes 3853496 | solution.py:45
  965.9 105.6 %while.55 = (s32[]{:T(128)}, f32[2,64,128]{2,1,0:T(8,128)}, bf16[2,64,128]{2,1,0:T(8,128)(2,1)S(1)}, f32[2]{0:T(128)S(1)}, f32[2,64,128]{2,1,0:T(8,128)S(1)}, /*index=5*/s32[]{:T(128)}) while((s32[]{:T(128)}, f32[2,64,128]{2,1,0:T(8,128)}, bf16[2,64,128]{2,1,0:T(8,128)(2,1)S(1)}, f32[2]{0:T(128)S(1)}, f32[2,64,128]{2,1,0:T(8,128)S(1)}, ...), condition=%wide.region_15.16_spmd, body=%wide.region_14.15_spmd.sunk | while | flops 65538 | bytes 327797 | solution.py:57
  968.8 7.4 collective-permute-start.1
  977.9 3.6 collective-permute-start.1
  983.1 5.4 collective-permute-start.1
  990.2 5.7 collective-permute-start.1
  997.6 5.7 collective-permute-start.1
  1005.0 5.7 collective-permute-start.1
  1012.4 5.9 collective-permute-start.1
  1019.9 5.6 collective-permute-start.1
  1027.1 5.7 collective-permute-start.1
  1034.5 5.7 collective-permute-start.1
  1041.9 5.7 collective-permute-start.1
  1049.3 5.7 collective-permute-start.1
  1056.7 5.7 collective-permute-start.1
  1064.1 5.7 collective-permute-start.1
  1071.5 3.6 fusion.62
  1077.5 3.4 copy.82
  1084.4 55.2 %psum.7 = bf16[8192]{0:T(1024)(128)(2,1)S(1)} all-reduce(bf16[8192]{0:T(1024)(128)(2,1)S(1)} %multiply_reduce_fusion), channel_id=1, replica_groups=mesh['seq'=16,'head'=8] {'head'}, use_global_device_ids=true, to_apply=%region_17.18 | all-reduce | flops 8192 | bytes 32768 | tf_op jit(solution)/shard_map/psum | solution.py:104
  1139.6 8.6 convolution_convert_fusion
  1148.3 64.9 %reduce-scatter.2.cloned.1.call-done = bf16[1024,512]{1,0:T(8,128)(2,1)} async-done(((bf16[8192,512]{1,0:T(8,128)(2,1)}), bf16[1024,512]{1,0:T(8,128)(2,1)}) %reduce-scatter.2.cloned.1.call-update) | async-done | bytes 1048592 | tf_op jit(solution)/shard_map/reduce_scatter | solution.py:109
  (406 shorter events, 264.9 us)
Async XLA Ops:
  6.5 1133.1 %copy-start = (bf16[128,512]{1,0:T(8,128)(2,1)S(1)}, bf16[128,512]{1,0:T(8,128)(2,1)}, u32[]{:S(2)}) copy-start(bf16[128,512]{1,0:T(8,128)(2,1)} %param.33) | copy-start | bytes 393220
  130.1 4.9 collective-permute-start
  135.7 4.6 collective-permute-start
  141.0 4.6 collective-permute-start
  146.3 4.6 collective-permute-start
  151.6 5.2 collective-permute-start
  157.4 6.8 collective-permute-start
  164.8 6.8 collective-permute-start
  172.2 6.8 collective-permute-start
  179.6 6.9 collective-permute-start
  187.1 6.6 collective-permute-start
  194.4 6.8 collective-permute-start
  201.8 6.8 collective-permute-start
  209.2 6.8 collective-permute-start
  216.6 6.8 collective-permute-start
  224.0 6.8 collective-permute-start
  260.2 16.6 %copy-start.2 = (s32[8192]{0:T(1024)S(1)}, s32[8192]{0:T(1024)}, u32[]{:S(2)}) copy-start(s32[8192]{0:T(1024)} %param.26) | copy-start | bytes 98308
  260.2 477.3 %all-to-all-start = ((bf16[16,8192,128]{2,1,0:T(8,128)(2,1)}), bf16[16,8192,128]{2,1,0:T(8,128)(2,1)}, u32[]{:S(2)}, u32[]{:S(2)}) async-start(bf16[16,8192,128]{2,1,0:T(8,128)(2,1)} %stack.3), calls=%async_computation | async-start | bytes 67108864 | tf_op jit(solution)/shard_map/all_to_all | solution.py:96
  276.6 936.6 %reduce-scatter.2.cloned.1.call-start = ((), (), s32[]{:S(2)}) async-start(), calls=%async_computation.2 | async-start | bytes 9437184 | tf_op jit(solution)/shard_map/reduce_scatter | solution.py:109
  965.9 2.3 collective-permute-start.1
  968.8 8.4 collective-permute-start.1
  977.9 4.6 collective-permute-start.1
  983.1 6.4 collective-permute-start.1
  990.2 6.8 collective-permute-start.1
  997.6 6.8 collective-permute-start.1
  1005.0 6.8 collective-permute-start.1
  1012.4 6.9 collective-permute-start.1
  1019.9 6.6 collective-permute-start.1
  1027.1 6.8 collective-permute-start.1
  1034.5 6.8 collective-permute-start.1
  1041.9 6.8 collective-permute-start.1
  1049.3 6.8 collective-permute-start.1
  1056.7 6.8 collective-permute-start.1
  1064.1 6.8 collective-permute-start.1
  1081.0 2.0 copy-start.1
  1082.9 56.7 %copy-start.3 = (f32[128]{0:T(128)S(1)}, f32[128]{0:T(128)}, u32[]{:S(2)}) copy-start(f32[128]{0:T(128)} %param.32) | copy-start | bytes 1540
Sparse Core Ops, SparseCore 0:
  1148.4 64.7 reduce-scatter.1
